TPU v7x, 32 devices: a whole 2x2x4 slice. The times are simulated.
32 devices in a mesh: row: 2 (over core), col: 4 (over z), ind: 4 (over y, x).
Axes of the slice: x: 2, y: 2, z: 4, core: 2. Of those that a mesh axis runs over, the one named last changes fastest.
Arguments:
- dosages: bfloat16 [4096, 1024], P('ind', ('row', 'col'))
- annotations: bfloat16 [1024, 1024], P('ind', ('row', 'col')), may hold values from -6 to 6
- window_end: int32 [1024], P(('row', 'col')), may hold values from 512 to 1024, as said below
Outputs:
- ld_scores: float32 [1024, 1024], P('ind', ('row', 'col'))
Inputs may be any that keep to these rules, and one draw needn't show every extreme that they name: window_end is nondecreasing, window_end[j] > j, and window_end[j] <= min(1024, (j // 128 + 4) * 128), the last bound reached in every draw.
All inputs are finite; a program needn't handle non-finite values.
Results may differ from a plain program's by a relative error of at most 0.0029.
Values may be sent and summed in bfloat16 or wider, within the bound.
A program may use at most 64 MiB of HBM per device.

v0:
```python
import jax
import jax.numpy as jnp
from jax import lax
from jax.sharding import PartitionSpec as P


def from_behind(array, axis, by):
    count = lax.axis_size(axis)
    pairs = [(i, i + by) for i in range(count) if 0 <= i + by < count]
    return lax.ppermute(array, axis, pairs)


def per_device(dosages, annotations, window_end):
    band_count = lax.axis_size("col")
    column_index = lax.axis_index("col")
    tile_size = dosages.shape[1]
    ind_rows = dosages.shape[0]
    ann_rows = annotations.shape[0]
    group_width = band_count * tile_size
    sample_count = ind_rows * lax.axis_size("ind")
    window_ends = lax.all_gather(window_end, "col", axis=0, tiled=True)
    group_x, group_a = (
        lax.all_gather(dosages, "col", axis=1, tiled=True),
        lax.all_gather(annotations, "col", axis=1, tiled=True),
    )
    next_x, next_a = from_behind((group_x, group_a), "row", -1)
    wide_x = jnp.concatenate([group_x, next_x], axis=1)
    wide_a = jnp.concatenate([group_a, next_a], axis=1)
    band_x = lax.dynamic_slice_in_dim(wide_x, column_index * tile_size, group_width, 1)
    band_a = lax.dynamic_slice_in_dim(wide_a, column_index * tile_size, group_width, 1)
    rows_x = group_x.reshape(ind_rows, band_count, tile_size)
    cols_x = band_x.reshape(ind_rows, band_count, tile_size)
    partial_gram = jnp.einsum("inb,ine->nbe", rows_x, cols_x, preferred_element_type=jnp.float32)
    gram = lax.psum(partial_gram, "ind")
    correlation_matrix = gram / sample_count
    raw_rsquared = correlation_matrix * correlation_matrix
    unbiased_rsquared = raw_rsquared - (1.0 - raw_rsquared) / (sample_count - 2)
    group_start = lax.axis_index("row") * group_width
    block_ids = jnp.arange(band_count, dtype=jnp.int32)[:, None, None]
    within_window = jnp.arange(tile_size, dtype=jnp.int32)
    row_pos = group_start + block_ids * tile_size + within_window[None, :, None]
    col_pos = group_start + (block_ids + column_index) * tile_size + within_window[None, None, :]
    limit = window_ends.reshape(band_count, tile_size)[:, :, None]
    inside = col_pos < limit
    upper = jnp.where((col_pos >= row_pos) & inside, unbiased_rsquared, 0.0).astype(jnp.bfloat16)
    strict = jnp.where((col_pos > row_pos) & inside, unbiased_rsquared, 0.0).astype(jnp.bfloat16)
    annotation_rows = group_a.reshape(ann_rows, band_count, tile_size)
    cols_a = band_a.reshape(ann_rows, band_count, tile_size)
    direct = jnp.einsum("cne,nae->cna", cols_a, upper, preferred_element_type=jnp.float32)
    mirror = jnp.einsum("cna,nae->cne", annotation_rows, strict, preferred_element_type=jnp.float32)
    direct = direct.reshape(ann_rows, group_width)
    mirror = mirror.reshape(ann_rows, group_width)
    window_acc = jnp.zeros((ann_rows, 2 * group_width), jnp.float32)
    window_acc = lax.dynamic_update_slice_in_dim(window_acc, mirror, column_index * tile_size, 1)
    window_acc = window_acc.at[:, :group_width].add(direct)
    incoming = from_behind(window_acc[:, group_width:], "row", 1)
    combined = window_acc[:, :group_width] + incoming
    ld_scores = lax.psum_scatter(combined, "col", scatter_dimension=1, tiled=True)
    return ld_scores


def solution(mesh):
    in_specs = (P("ind", ("row", "col")), P("ind", ("row", "col")), P(("row", "col")))
    out_specs = P("ind", ("row", "col"))
    return jax.shard_map(
        per_device, mesh=mesh, in_specs=in_specs, out_specs=out_specs, check_vma=False
    )
```

profile of v0, /device:TPU:1, one launch (start us, length us, event | category | flops | bytes accessed | tf_op | source)
XLA Modules:
  0.0 137.0 jit_solution(7500563988074717324)
XLA Ops:
  6.5 0.0 all-gather.3.cloned.1.call-start
  6.5 1.8 %copy.16 = bf16[1024,128]{0,1:T(8,128)(2,1)} copy(bf16[1024,128]{1,0:T(8,128)(2,1)} %param.5) | data formatting | bytes 524288 | tf_op args[0]
  8.3 0.0 all-gather.3.cloned.1.call-update
  8.4 0.0 all-reduce.2.cloned.1.call-start
  8.4 30.1 %all-gather.3.cloned.1.call-done = bf16[1024,512]{0,1:T(8,128)(2,1)} async-done(((bf16[1024,128]{0,1:T(8,128)(2,1)}), bf16[1024,512]{0,1:T(8,128)(2,1)}) %all-gather.3.cloned.1.call-update) | async-done | bytes 1048592 | tf_op jit(solution)/shard_map/all_gather | solution.py:23
  38.5 3.1 %collective-permute-start = (bf16[1024,512]{0,1:T(8,128)(2,1)}, bf16[1024,512]{0,1:T(8,128)(2,1)S(1)}, u32[]{:S(2)}, u32[]{:S(2)}) collective-permute-start(bf16[1024,512]{0,1:T(8,128)(2,1)} %all-gather.3.cloned.1.call-done), channel_id=1, source_target_pairs={{16,0},{17,1},{18,2},{19,3},{20,4},{21,5},{22,6},{23,7},{24,8},{25... | collective-permute-start | bytes 3145736 | tf_op jit(solution)/shard_map/ppermute | solution.py:10
  41.6 0.9 copy.18
  42.6 12.4 %all_gather.11 = bf16[256,512]{0,1:T(8,128)(2,1)S(1)} all-gather(bf16[256,128]{0,1:T(8,128)(2,1)S(1)} %copy.18), channel_id=1, replica_groups=mesh['row'=2,'col'=4,'ind'=4] {'col'}, dimensions={1}, use_global_device_ids=true | all-gather | bytes 327680 | tf_op jit(solution)/shard_map/all_gather | solution.py:24
  54.9 3.2 %collective-permute-start.1 = (bf16[256,512]{0,1:T(8,128)(2,1)S(1)}, bf16[256,512]{0,1:T(8,128)(2,1)S(1)}, u32[]{:S(2)}, u32[]{:S(2)}) collective-permute-start(bf16[256,512]{0,1:T(8,128)(2,1)S(1)} %all_gather.11), channel_id=1, source_target_pairs={{16,0},{17,1},{18,2},{19,3},{20,4},{21,5},{22,6},{23,7},{24,8},{25... | collective-permute-start | bytes 786440 | tf_op jit(solution)/shard_map/ppermute | solution.py:10
  58.2 0.0 copy-start
  58.2 0.0 collective-permute-done
  58.2 2.3 %fusion = bf16[1024,512]{0,1:T(8,128)(2,1)S(1)} fusion(s32[]{:T(128)S(6)} %select_n.12, bf16[1024,512]{0,1:T(8,128)(2,1)} %all-gather.3.cloned.1.call-done, bf16[1024,512]{0,1:T(8,128)(2,1)S(1)} %collective-permute-done), kind=kLoop, calls=%fused_computation.3 | loop fusion | flops 2097152 | bytes 3145732 | tf_op jit(solution)/shard_map/concatenate | solution.py:27
  60.5 0.0 copy-done
  60.5 0.0 copy-start.2
  60.5 1.1 convolution_bitcast_fusion
  61.7 0.0 all-reduce.2.cloned.1.call-update
  61.7 0.0 reduce-scatter.2.cloned.1.call-start
  61.8 0.1 iota_add_fusion
  61.8 0.0 copy-done.2
  61.8 7.1 %all-gather = s32[4,1,128]{2,1,0:T(1,128)S(1)} all-gather(s32[1,1,128]{2,1,0:T(1,128)S(1)} %bitcast.26), channel_id=1, replica_groups=mesh['row'=2,'col'=4,'ind'=4] {'col'}, dimensions={0}, use_global_device_ids=true | all-gather | bytes 2560 | tf_op jit(solution)/shard_map/all_gather | solution.py:21
  68.9 0.1 iota_add_fusion.1
  69.0 34.1 %all-reduce.2.cloned.1.call-done = f32[4,128,128]{1,2,0:T(8,128)} async-done(((f32[4,128,128]{1,2,0:T(8,128)}), f32[4,128,128]{1,2,0:T(8,128)}) %all-reduce.2.cloned.1.call-update) | async-done | bytes 262160 | tf_op jit(solution)/shard_map/psum | solution.py:34
  103.0 1.2 fusion.3
  104.2 0.2 copy.20
  104.5 0.1 broadcast_in_dim.11
  104.6 0.1 constant_dynamic-update-slice_fusion
  104.6 0.0 copy-start.1
  104.7 1.4 %collective-permute-start.2 = (f32[256,512]{1,0:T(8,128)S(1)}, f32[256,512]{1,0:T(8,128)S(1)}, u32[]{:S(2)}, u32[]{:S(2)}) collective-permute-start(f32[256,512]{1,0:T(8,128)S(1)} %slice.29), channel_id=1, source_target_pairs={{0,16},{1,17},{2,18},{3,19},{4,20},{5,21},{6,22},{7,23},{8,24},{9,... | collective-permute-start | bytes 1572872 | tf_op jit(solution)/shard_map/ppermute | solution.py:10
  106.1 0.6 compare_reduce_fusion
  106.8 0.0 collective-permute-done.1
  106.8 0.6 fusion.2
  107.4 0.0 copy-done.1
  107.4 0.4 fusion.4
  107.8 0.2 copy.23
  108.0 0.7 collective-permute-done.2
  108.7 1.6 %fusion.1 = f32[256,512]{1,0:T(8,128)} fusion(f32[256,512]{1,0:T(8,128)S(1)} %collective-permute-done.2, f32[256,512]{1,0:T(8,128)S(1)} %copy.23, f32[256,1024]{1,0:T(8,128)S(1)} %constant_dynamic-update-slice_fusion, pred[]{:T(512)} %compare_reduce_fusion), kind=kLoop, calls=%fused_computation.5 | loop fusion | flops 393216 | bytes 2097153 | tf_op jit(solution)/shard_map/add | solution.py:57
  110.2 0.0 reduce-scatter.2.cloned.1.call-update
  110.3 20.2 %reduce-scatter.2.cloned.1.call-done = f32[256,128]{1,0:T(8,128)} async-done(((f32[256,512]{1,0:T(8,128)}), f32[256,128]{1,0:T(8,128)}) %reduce-scatter.2.cloned.1.call-update) | async-done | bytes 131088 | tf_op jit(solution)/shard_map/reduce_scatter | solution.py:58
  (2 shorter events, 0.0 us)
Async XLA Ops:
  6.5 32.0 %all-gather.3.cloned.1.call-start = ((), (), s32[]{:S(2)}) async-start(), calls=%async_computation.1 | async-start | bytes 1310720 | tf_op jit(solution)/shard_map/all_gather | solution.py:23
  8.4 94.7 %all-reduce.2.cloned.1.call-start = ((), (), s32[]{:S(2)}) async-start(), calls=%async_computation.2 | async-start | bytes 524288 | tf_op jit(solution)/shard_map/psum | solution.py:34
  38.5 19.7 %collective-permute-start = (bf16[1024,512]{0,1:T(8,128)(2,1)}, bf16[1024,512]{0,1:T(8,128)(2,1)S(1)}, u32[]{:S(2)}, u32[]{:S(2)}) collective-permute-start(bf16[1024,512]{0,1:T(8,128)(2,1)} %all-gather.3.cloned.1.call-done), channel_id=1, source_target_pairs={{16,0},{17,1},{18,2},{19,3},{20,4},{21,5},{22,6},{23,7},{24,8},{25... | collective-permute-start | bytes 3145736 | tf_op jit(solution)/shard_map/ppermute | solution.py:10
  54.9 51.8 %collective-permute-start.1 = (bf16[256,512]{0,1:T(8,128)(2,1)S(1)}, bf16[256,512]{0,1:T(8,128)(2,1)S(1)}, u32[]{:S(2)}, u32[]{:S(2)}) collective-permute-start(bf16[256,512]{0,1:T(8,128)(2,1)S(1)} %all_gather.11), channel_id=1, source_target_pairs={{16,0},{17,1},{18,2},{19,3},{20,4},{21,5},{22,6},{23,7},{24,8},{25... | collective-permute-start | bytes 786440 | tf_op jit(solution)/shard_map/ppermute | solution.py:10
  58.2 2.3 %copy-start = (bf16[1024,512]{0,1:T(8,128)(2,1)S(1)}, bf16[1024,512]{0,1:T(8,128)(2,1)}, u32[]{:S(2)}) copy-start(bf16[1024,512]{0,1:T(8,128)(2,1)} %all-gather.3.cloned.1.call-done) | copy-start | bytes 3145732
  60.5 1.3 copy-start.2
  61.7 68.7 %reduce-scatter.2.cloned.1.call-start = ((), (), s32[]{:S(2)}) async-start(), calls=%async_computation.3 | async-start | bytes 655360 | tf_op jit(solution)/shard_map/reduce_scatter | solution.py:58
  104.6 2.8 %copy-start.1 = (f32[4,128,128]{1,2,0:T(8,128)S(1)}, f32[4,128,128]{1,2,0:T(8,128)}, u32[]{:S(2)}) copy-start(f32[4,128,128]{1,2,0:T(8,128)} %all-reduce.2.cloned.1.call-done) | copy-start | bytes 786436
  104.7 4.0 %collective-permute-start.2 = (f32[256,512]{1,0:T(8,128)S(1)}, f32[256,512]{1,0:T(8,128)S(1)}, u32[]{:S(2)}, u32[]{:S(2)}) collective-permute-start(f32[256,512]{1,0:T(8,128)S(1)} %slice.29), channel_id=1, source_target_pairs={{0,16},{1,17},{2,18},{3,19},{4,20},{5,21},{6,22},{7,23},{8,24},{9,... | collective-permute-start | bytes 1572872 | tf_op jit(solution)/shard_map/ppermute | solution.py:10
Sparse Core Ops, SparseCore 0:
  8.9 29.5 all-gather.2
  61.8 41.1 all-reduce.1
  110.4 19.9 reduce-scatter.1
where the time goes:
time: 140 us; the launch traced here: 137 us
  waiting for transfers between devices  85.1 us (61%)
  blocking collectives  19.4 us (14%)
  between operations  13.3 us (10%)
  starting transfers between devices  7.86 us (6%)
  other arithmetic  5.3 us (4%)
  local copies, waits for them, and re-layouts  3.34 us (2%)
  matrix products  2.71 us (2%)
    psum x1, waiting for transfers between devices, per_device(): gram = lax.psum(partial_gram, 'ind')  34.1 us
    all_gather x1, waiting for transfers between devices, per_device(): lax.all_gather(dosages, 'col', axis=1, tiled=True)  30.1 us
    reduce_scatter x1, waiting for transfers between devices, per_device(): lax.psum_scatter(combined, 'col', scatter_dimension=1, tiled=True)  20.2 us
    all_gather x1, blocking collectives, per_device(): lax.all_gather(annotations, 'col', axis=1, tiled=True)  12.4 us
    ppermute x3, starting transfers between devices, from_behind(): return lax.ppermute(array, axis, pairs)  7.78 us
    all_gather x1, blocking collectives, per_device(): window_ends = lax.all_gather(window_end, 'col', axis=0, tiled=True)  7.07 us
  transfers between devices with their start and end apart: 6, of which 4 were waited for; matrix products, arithmetic and copies ran while one was open for 6% of the time, Pallas kernels for 0%

commit v1 on v0

v1 whole, which is shorter than its diff:
```python
import functools

import jax
import jax.numpy as jnp
from jax import lax
from jax.experimental import pallas as pl
from jax.experimental.pallas import tpu as pltpu
from jax.sharding import PartitionSpec as P

MESH = pl.DeviceIdType.MESH


def kernel(rows, cols, inds, samples, x_ref, a_ref, w_ref, o_ref, xs, xn, xt, nt, wl, wc,
           gp, rs, sq, sm, am, sems):
    (load_sem, xsend, xrecv, nsend, nrecv, wsend, wrecv, aup, adn, axs, arecv, crecv,
     rsend, rrecv, ssend, srecv) = sems
    r, c, i = lax.axis_index("row"), lax.axis_index("col"), lax.axis_index("ind")
    tile = x_ref.shape[1]
    part = tile // inds
    last = r == rows - 1
    toward = jnp.where(last, -1, 1)
    arrivals = jnp.where(last, c, cols - 1 - c)
    nxt = c - toward
    has_next = (nxt >= 0) & (nxt < cols)
    has_row_below = r < rows - 1
    has_row_above = r > 0

    def dev(row, col, ind):
        return {"row": row, "col": col, "ind": ind}

    def remote(src, dst, send, recv, target):
        return pltpu.make_async_remote_copy(
            src_ref=src, dst_ref=dst, send_sem=send, recv_sem=recv,
            device_id=target, device_id_type=MESH)

    def when(cond, fn):
        pl.when(cond)(fn)

    def loop(lo, hi, fn):
        def body(step, carry):
            fn(step)
            return carry
        lax.fori_loop(lo, hi, body, 0)

    barrier = pltpu.get_barrier_semaphore()

    def greet(row, col, ind):
        pl.semaphore_signal(barrier, inc=1, device_id=dev(row, col, ind), device_id_type=MESH)

    def greet_col(col):
        def each(k):
            ind = lax.rem(i + k, inds)
            when((col != c) | (k > 0), lambda: greet(r, col, ind))
            when((col < c) & has_row_below, lambda: greet(r + 1, col, ind))
            when((col > c) & has_row_above, lambda: greet(r - 1, col, ind))
            when((col == c) & has_row_below, lambda: greet(r + 1, col, ind))
            when((col == c) & has_row_above, lambda: greet(r - 1, col, ind))
        loop(0, inds, each)

    loop(0, cols, greet_col)
    below = has_row_below.astype(jnp.int32)
    above = has_row_above.astype(jnp.int32)
    peers = cols + below * (c + 1) + above * (cols - c)
    pl.semaphore_wait(barrier, peers * inds - 1)

    def send_x(slot, src):
        return remote(src, xs.at[slot + 1], xsend.at[slot], xrecv.at[slot + 1], dev(r, nxt, i))

    send_up_row = remote(x_ref, xn, nsend.at[0], nrecv.at[0], dev(r - 1, c, i))

    def send_w(step):
        return remote(w_ref, wl.at[c], wsend.at[step], wrecv.at[c],
                      dev(r, c - toward * step, i))

    def a_up(col, src):
        return remote(src, am.at[0, col], aup.at[col], arecv.at[col], dev(r, c + 1, i))

    def a_down(col, src):
        return remote(src, am.at[0, col], adn.at[col], arecv.at[col], dev(r, c - 1, i))

    def a_cross(col, row):
        return remote(am.at[0, col], am.at[1, col], axs.at[col], crecv.at[col], dev(row, c, i))

    when(has_next, lambda: send_x(0, x_ref).start())
    when(has_row_above, lambda: send_up_row.start())
    load_x = pltpu.make_async_copy(x_ref, xs.at[0], load_sem.at[0])
    load_x.start()
    load_a = pltpu.make_async_copy(a_ref, am.at[0, c], load_sem.at[1])
    load_a.start()
    w_count = cols - 1 - arrivals
    loop(1, w_count + 1, lambda step: send_w(step).start())
    when(c + 1 < cols, lambda: a_up(c, a_ref).start())
    when(c > 0, lambda: a_down(c, a_ref).start())

    w_own = w_ref[...]
    wl[c] = w_own
    wide = jnp.broadcast_to(w_own.astype(jnp.float32), (tile, tile))
    wc[...] = wide.T.astype(jnp.int32).reshape(inds, part, tile)

    def reduce_send(t, k):
        to = lax.rem(i + k, inds)
        return remote(gp.at[t, to], rs.at[k - 1, t], rsend.at[k - 1, t], rrecv.at[k - 1, t],
                      dev(r, c, to))

    def put_tile(t, value):
        gp[t] = value.reshape(inds, part, tile)
        loop(1, inds, lambda k: reduce_send(t, k).start())

    load_x.wait()
    xt[...] = xs[0].T
    put_tile(0, jnp.dot(xt[...], xs[0], preferred_element_type=jnp.float32))

    def take_next_row():
        send_up_row.wait_recv()
        nt[...] = xn[...].T

    when(has_row_below, take_next_row)

    row_iota = lax.broadcasted_iota(jnp.int32, (part, tile), 0) + i * part
    lane_iota = lax.broadcasted_iota(jnp.int32, (part, tile), 1)

    def s_send(t, which, k, kind, row, col, slot):
        to = lax.rem(i + k, inds)
        return remote(sq.at[t], sm.at[kind, slot, i], ssend.at[t, which, k],
                      srecv.at[kind, slot, i], dev(row, col, to))

    def total_of(t):
        total = gp[t, i]
        for k in range(1, inds):
            reduce_send(t, k).wait_recv()
            total = total + rs[k - 1, t]
        corr = total / samples
        rsq = corr * corr
        return rsq - (1.0 - rsq) / (samples - 2)

    def finish_diag():
        adj = total_of(0)
        base = (r * cols + c) * tile
        ahead = lane_iota >= row_iota
        pos = base + jnp.where(ahead, lane_iota, row_iota)
        lim = jnp.where(ahead, wc[i], jnp.broadcast_to(wl[c], (part, tile)))
        val = jnp.where(pos < lim, adj, 0.0).astype(jnp.bfloat16)
        sq[0] = val
        sm[0, c, i] = val
        loop(1, inds, lambda k: s_send(0, 0, k, 0, r, c, c).start())

    def finish_same(s):
        col = c + toward * s
        adj = total_of(s)
        pos = jnp.where(last, (r * cols + c) * tile + row_iota, (r * cols + col) * tile + lane_iota)
        lim = jnp.where(last, jnp.broadcast_to(wl[col], (part, tile)), wc[i])
        val = jnp.where(pos < lim, adj, 0.0).astype(jnp.bfloat16)
        sq[s] = val
        sm[0, col, i] = val
        loop(0, inds, lambda k: s_send(s, 1, k, 0, r, col, c).start())
        loop(1, inds, lambda k: s_send(s, 0, k, 0, r, c, col).start())

    def finish_cross(s):
        col = c + toward * s
        t = cols - 1 + s
        adj = total_of(t)
        pos = ((r + 1) * cols + c) * tile + row_iota
        lim = jnp.broadcast_to(wl[col], (part, tile))
        sq[t] = jnp.where(pos < lim, adj, 0.0).astype(jnp.bfloat16)
        loop(0, inds, lambda k: s_send(t, 1, k, 1, r, col, c).start())
        loop(0, inds, lambda k: s_send(t, 0, k, 1, r + 1, c, col).start())

    def finish(s):
        col = c + toward * s
        remote(w_ref, wl.at[col], wsend.at[0], wrecv.at[col], dev(r, nxt, i)).wait_recv()
        finish_same(s)
        when(has_row_below, lambda: finish_cross(s))

    def pass_a(s):
        def from_below():
            col = c - s
            a_up(col, am.at[0, col]).wait_recv()
            when(c + 1 < cols, lambda: a_up(col, am.at[0, col]).start())
            when(has_row_above, lambda: a_cross(col, r - 1).start())

        def from_above():
            col = c + s
            a_down(col, am.at[0, col]).wait_recv()
            when(c > 0, lambda: a_down(col, am.at[0, col]).start())
            when(has_row_below, lambda: a_cross(col, r + 1).start())

        when(c - s >= 0, from_below)
        when(c + s < cols, from_above)

    def step_x(s):
        send_x(s - 1, xs.at[s - 1]).wait_recv()
        when(has_next, lambda: send_x(s, xs.at[s]).start())
        put_tile(s, jnp.dot(xt[...], xs[s], preferred_element_type=jnp.float32))
        when(has_row_below, lambda: put_tile(
            cols - 1 + s, jnp.dot(nt[...], xs[s], preferred_element_type=jnp.float32)))

    def step(s):
        when(s <= arrivals, lambda: step_x(s))
        pass_a(s)
        when(s == 1, finish_diag)
        when((s >= 2) & (s - 1 <= arrivals), lambda: finish(s - 1))

    loop(1, cols, step)
    when(arrivals == cols - 1, lambda: finish(cols - 1))

    load_a.wait()

    def take(kind, slot, q):
        remote(sq.at[0], sm.at[kind, slot, q], ssend.at[0, 0, 0], srecv.at[kind, slot, q],
               dev(r, c, lax.rem(i + 1, inds))).wait_recv()

    def add(kind, slot, flip):
        lhs = am[kind, slot]
        rhs = sm[kind, slot].reshape(tile, tile)
        dims = (((1,), (1,)), ((), ())) if flip else (((1,), (0,)), ((), ()))
        o_ref[...] += lax.dot_general(lhs, rhs, dims, preferred_element_type=jnp.float32)

    loop(1, inds, lambda k: take(0, c, lax.rem(i + k, inds)))
    o_ref[...] = lax.dot_general(am[0, c], sm[0, c].reshape(tile, tile),
                                 (((1,), (0,)), ((), ())), preferred_element_type=jnp.float32)

    def add_home(s):
        col = c + toward * s
        loop(1, inds, lambda k: take(0, col, lax.rem(i + k, inds)))
        add(0, col, True)

    loop(1, arrivals + 1, add_home)

    def add_away(s):
        col = c - toward * s
        loop(0, inds, lambda q: take(0, col, q))
        add(0, col, False)

    loop(1, w_count + 1, add_away)

    def add_cross(col):
        a_cross_wait = remote(am.at[0, col], am.at[1, col], axs.at[col], crecv.at[col],
                              dev(r, nxt, i))
        a_cross_wait.wait_recv()
        loop(0, inds, lambda q: take(1, col, q))
        when(col < c, lambda: add(1, col, False))
        when(col > c, lambda: add(1, col, True))

    when(has_row_below, lambda: loop(0, c, add_cross))
    when(has_row_above, lambda: loop(c + 1, cols, add_cross))

    when(has_next, lambda: loop(0, arrivals + 1, lambda s: send_x(s, xs.at[s]).wait_send()))
    when(has_row_above, lambda: send_up_row.wait_send())
    loop(1, w_count + 1, lambda s: send_w(s).wait_send())
    when(c + 1 < cols, lambda: loop(0, c + 1, lambda q: a_up(q, am.at[0, q]).wait_send()))
    when(c > 0, lambda: loop(c, cols, lambda q: a_down(q, am.at[0, q]).wait_send()))
    when(has_row_above, lambda: loop(0, c, lambda q: a_cross(q, r - 1).wait_send()))
    when(has_row_below, lambda: loop(c + 1, cols, lambda q: a_cross(q, r + 1).wait_send()))

    def drain(t, kind, row, col):
        loop(1, inds, lambda k: reduce_send(t, k).wait_send())
        loop(0, inds, lambda k: s_send(t, 1, k, kind, r, col, c).wait_send())

    loop(1, inds, lambda k: reduce_send(0, k).wait_send())
    loop(1, inds, lambda k: s_send(0, 0, k, 0, r, c, c).wait_send())

    def drain_step(s):
        col = c + toward * s
        drain(s, 0, r, col)
        loop(1, inds, lambda k: s_send(s, 0, k, 0, r, c, col).wait_send())

        def cross():
            drain(cols - 1 + s, 1, r, col)
            loop(0, inds, lambda k: s_send(cols - 1 + s, 0, k, 1, r + 1, c, col).wait_send())

        when(has_row_below, cross)

    loop(1, arrivals + 1, drain_step)


def per_device(rows, cols, inds, dosages, annotations, window_end):
    depth, tile = dosages.shape
    ann = annotations.shape[0]
    samples = depth * inds
    part = tile // inds
    tiles = 2 * cols - 1
    dma = pltpu.SemaphoreType.DMA
    sems = (dma((2,)), dma((cols,)), dma((cols,)), dma((1,)), dma((1,)), dma((cols,)),
            dma((cols,)), dma((cols,)), dma((cols,)), dma((cols,)), dma((cols,)), dma((cols,)),
            dma((inds - 1, tiles)), dma((inds - 1, tiles)), dma((tiles, 2, inds)),
            dma((2, cols, inds)))
    return pl.pallas_call(
        functools.partial(kernel, rows, cols, inds, samples),
        out_shape=jax.ShapeDtypeStruct((ann, tile), jnp.float32),
        in_specs=[pl.BlockSpec(memory_space=pl.ANY), pl.BlockSpec(memory_space=pl.ANY),
                  pl.BlockSpec(memory_space=pltpu.VMEM)],
        out_specs=pl.BlockSpec(memory_space=pltpu.VMEM),
        scratch_shapes=[
            pltpu.VMEM((cols, depth, tile), jnp.bfloat16),
            pltpu.VMEM((depth, tile), jnp.bfloat16),
            pltpu.VMEM((tile, depth), jnp.bfloat16),
            pltpu.VMEM((tile, depth), jnp.bfloat16),
            pltpu.VMEM((cols, 1, tile), jnp.int32),
            pltpu.VMEM((inds, part, tile), jnp.int32),
            pltpu.VMEM((tiles, inds, part, tile), jnp.float32),
            pltpu.VMEM((inds - 1, tiles, part, tile), jnp.float32),
            pltpu.VMEM((tiles, part, tile), jnp.bfloat16),
            pltpu.VMEM((2, cols, inds, part, tile), jnp.bfloat16),
            pltpu.VMEM((2, cols, ann, tile), jnp.bfloat16),
            sems,
        ],
        compiler_params=pltpu.CompilerParams(collective_id=0, has_side_effects=True),
    )(dosages, annotations, window_end.reshape(1, tile))


def solution(mesh):
    in_specs = (P("ind", ("row", "col")), P("ind", ("row", "col")), P(("row", "col")))
    out_specs = P("ind", ("row", "col"))
    body = functools.partial(per_device, mesh.shape["row"], mesh.shape["col"], mesh.shape["ind"])
    return jax.shard_map(body, mesh=mesh, in_specs=in_specs, out_specs=out_specs, check_vma=False)
```

time: 140 us -> 35.4 us (0.25)
  the two profiles are of different devices: /device:TPU:1 before, /device:TPU:0 now
where the time goes in v1:
time: 35.4 us; the launch traced here: 35.2 us
  Pallas kernels  33.6 us (95%)
  local copies, waits for them, and re-layouts  1.57 us (4%)
    pallas_call x1, Pallas kernels, per_device(): pl.pallas_call(functools.partial(kernel, rows, cols, inds, samples), out_...  33.6 us
    unnamed x1, local copies, waits for them, and re-layouts  1.57 us

profile of v1, /device:TPU:0, one launch (start us, length us, event | category | flops | bytes accessed | tf_op | source)
XLA Modules:
  0.0 35.2 jit_solution(6102365248143377357)
XLA Ops:
  0.0 33.6 %shard_map.37 = f32[256,128]{1,0:T(8,128)} custom-call(bf16[1024,128]{1,0:T(8,128)(2,1)} %x_ref.1, bf16[256,128]{1,0:T(8,128)(2,1)} %a_ref.1, s32[1,128]{1,0:T(1,128)} %bitcast.1), custom_call_target="tpu_custom_call" | custom-call | tf_op jit(solution)/shard_map/pallas_call | solution.py:287
  33.6 1.6 %copy.5 = f32[256,128]{1,0:T(8,128)} copy(f32[256,128]{1,0:T(8,128)} %shard_map.37) | data formatting | bytes 262144

commit v2 on v1

--- a/solution.py
+++ b/solution.py
@@ -47,30 +47,23 @@
     def greet(row, col, ind):
         pl.semaphore_signal(barrier, inc=1, device_id=dev(row, col, ind), device_id_type=MESH)
 
-    def greet_col(col):
-        def each(k):
-            ind = lax.rem(i + k, inds)
-            when((col != c) | (k > 0), lambda: greet(r, col, ind))
-            when((col < c) & has_row_below, lambda: greet(r + 1, col, ind))
-            when((col > c) & has_row_above, lambda: greet(r - 1, col, ind))
-            when((col == c) & has_row_below, lambda: greet(r + 1, col, ind))
-            when((col == c) & has_row_above, lambda: greet(r - 1, col, ind))
-        loop(0, inds, each)
-
-    loop(0, cols, greet_col)
-    below = has_row_below.astype(jnp.int32)
-    above = has_row_above.astype(jnp.int32)
-    peers = cols + below * (c + 1) + above * (cols - c)
-    pl.semaphore_wait(barrier, peers * inds - 1)
+    when(c > 0, lambda: greet(r, c - 1, i))
+    when(c + 1 < cols, lambda: greet(r, c + 1, i))
+    when(has_row_below, lambda: greet(r + 1, c, i))
+    when(has_row_above, lambda: greet(r - 1, c, i))
+    for k in range(1, inds):
+        greet(r, c, lax.rem(i + k, inds))
+    near = [c > 0, c + 1 < cols, has_row_below, has_row_above]
+    pl.semaphore_wait(barrier, inds - 1 + sum(n.astype(jnp.int32) for n in near))
 
     def send_x(slot, src):
         return remote(src, xs.at[slot + 1], xsend.at[slot], xrecv.at[slot + 1], dev(r, nxt, i))
 
     send_up_row = remote(x_ref, xn, nsend.at[0], nrecv.at[0], dev(r - 1, c, i))
 
-    def send_w(step):
-        return remote(w_ref, wl.at[c], wsend.at[step], wrecv.at[c],
-                      dev(r, c - toward * step, i))
+    def send_w(slot, src):
+        col = c + toward * slot
+        return remote(src, wl.at[col], wsend.at[slot], wrecv.at[col], dev(r, nxt, i))
 
     def a_up(col, src):
         return remote(src, am.at[0, col], aup.at[col], arecv.at[col], dev(r, c + 1, i))
@@ -87,8 +80,8 @@
     load_x.start()
     load_a = pltpu.make_async_copy(a_ref, am.at[0, c], load_sem.at[1])
     load_a.start()
-    w_count = cols - 1 - arrivals
-    loop(1, w_count + 1, lambda step: send_w(step).start())
+    away = cols - 1 - arrivals
+    when(has_next, lambda: send_w(0, w_ref).start())
     when(c + 1 < cols, lambda: a_up(c, a_ref).start())
     when(c > 0, lambda: a_down(c, a_ref).start())
 
@@ -166,8 +159,6 @@
         loop(0, inds, lambda k: s_send(t, 0, k, 1, r + 1, c, col).start())
 
     def finish(s):
-        col = c + toward * s
-        remote(w_ref, wl.at[col], wsend.at[0], wrecv.at[col], dev(r, nxt, i)).wait_recv()
         finish_same(s)
         when(has_row_below, lambda: finish_cross(s))
 
@@ -190,6 +181,8 @@
     def step_x(s):
         send_x(s - 1, xs.at[s - 1]).wait_recv()
         when(has_next, lambda: send_x(s, xs.at[s]).start())
+        send_w(s, wl.at[c + toward * s]).wait_recv()
+        when(has_next, lambda: send_w(s, wl.at[c + toward * s]).start())
         put_tile(s, jnp.dot(xt[...], xs[s], preferred_element_type=jnp.float32))
         when(has_row_below, lambda: put_tile(
             cols - 1 + s, jnp.dot(nt[...], xs[s], preferred_element_type=jnp.float32)))
@@ -231,7 +224,7 @@
         loop(0, inds, lambda q: take(0, col, q))
         add(0, col, False)
 
-    loop(1, w_count + 1, add_away)
+    loop(1, away + 1, add_away)
 
     def add_cross(col):
         a_cross_wait = remote(am.at[0, col], am.at[1, col], axs.at[col], crecv.at[col],
@@ -246,7 +239,7 @@
 
     when(has_next, lambda: loop(0, arrivals + 1, lambda s: send_x(s, xs.at[s]).wait_send()))
     when(has_row_above, lambda: send_up_row.wait_send())
-    loop(1, w_count + 1, lambda s: send_w(s).wait_send())
+    when(has_next, lambda: loop(0, arrivals + 1, lambda s: send_w(s, wl.at[c + toward * s]).wait_send()))
     when(c + 1 < cols, lambda: loop(0, c + 1, lambda q: a_up(q, am.at[0, q]).wait_send()))
     when(c > 0, lambda: loop(c, cols, lambda q: a_down(q, am.at[0, q]).wait_send()))
     when(has_row_above, lambda: loop(0, c, lambda q: a_cross(q, r - 1).wait_send()))

time: 35.4 us -> 34.3 us (0.969)
  Pallas kernels: 33.6 us -> 32.6 us
    pallas_call x1, Pallas kernels: 33.6 us -> 32.6 us  [per_device(): pl.pallas_call(functools.partial(kernel, rows, cols, inds, samples), out_...]
where the time goes in v2:
time: 34.3 us; the launch traced here: 34.1 us
  Pallas kernels  32.6 us (95%)
  local copies, waits for them, and re-layouts  1.57 us (5%)
    pallas_call x1, Pallas kernels, per_device(): pl.pallas_call(functools.partial(kernel, rows, cols, inds, samples), out_...  32.6 us
    unnamed x1, local copies, waits for them, and re-layouts  1.57 us

profile of v2, /device:TPU:0, one launch (start us, length us, event | category | flops | bytes accessed | tf_op | source)
XLA Modules:
  0.0 34.1 jit_solution(126129751445894399)
XLA Ops:
  0.0 32.6 %shard_map.37 = f32[256,128]{1,0:T(8,128)} custom-call(bf16[1024,128]{1,0:T(8,128)(2,1)} %x_ref.1, bf16[256,128]{1,0:T(8,128)(2,1)} %a_ref.1, s32[1,128]{1,0:T(1,128)} %bitcast.1), custom_call_target="tpu_custom_call" | custom-call | tf_op jit(solution)/shard_map/pallas_call | solution.py:280
  32.6 1.6 %copy.5 = f32[256,128]{1,0:T(8,128)} copy(f32[256,128]{1,0:T(8,128)} %shard_map.37) | data formatting | bytes 262144

commit v3 on v2

v3 whole, which is shorter than its diff:
```python
import functools

import jax
import jax.numpy as jnp
from jax import lax
from jax.experimental import pallas as pl
from jax.experimental.pallas import tpu as pltpu
from jax.sharding import PartitionSpec as P

MESH = pl.DeviceIdType.MESH


def kernel(rows, cols, inds, samples, x_ref, a_ref, w_ref, o_ref, xs, xn, xt, wl, wc,
           gp, rs, sq, sm, am, sems):
    (load_sem, xsend, xrecv, nsend, nrecv, wsend, wrecv, aup, adn, axs, arecv, crecv,
     rrecv, ssend, srecv) = sems
    r, c, i = lax.axis_index("row"), lax.axis_index("col"), lax.axis_index("ind")
    tile = x_ref.shape[1]
    part = tile // inds
    right_hub = cols // 2
    left_hub = right_hub - 1
    span = max(right_hub, cols - right_hub)
    last = r == rows - 1
    has_row_below = r < rows - 1
    has_row_above = r > 0
    main = jnp.where(last, right_hub, left_hub)
    is_main = c == main
    is_hub = (c == left_hub) | (c == right_hub)
    on_left = c <= left_hub
    low = jnp.where(on_left, 0, right_hub)
    high = jnp.where(on_left, left_hub, cols - 1)
    nxt = jnp.where(c < main, c + 1, c - 1)
    takes_left = c <= main
    takes_right = c >= main

    def dev(row, col, ind):
        return {"row": row, "col": col, "ind": ind}

    def remote(src, dst, send, recv, target):
        return pltpu.make_async_remote_copy(
            src_ref=src, dst_ref=dst, send_sem=send, recv_sem=recv,
            device_id=target, device_id_type=MESH)

    def when(cond, fn):
        pl.when(cond)(fn)

    def loop(lo, hi, fn):
        def body(step, carry):
            fn(step)
            return carry
        lax.fori_loop(lo, hi, body, 0)

    barrier = pltpu.get_barrier_semaphore()

    def greet(row, col, ind):
        pl.semaphore_signal(barrier, inc=1, device_id=dev(row, col, ind), device_id_type=MESH)

    when(c > 0, lambda: greet(r, c - 1, i))
    when(c + 1 < cols, lambda: greet(r, c + 1, i))
    when(has_row_below, lambda: greet(r + 1, c, i))
    when(has_row_above, lambda: greet(r - 1, c, i))
    for k in range(1, inds):
        greet(r, c, lax.rem(i + k, inds))
    load_x = pltpu.make_async_copy(x_ref, xs.at[c], load_sem.at[0])
    load_x.start()
    load_a = pltpu.make_async_copy(a_ref, am.at[0, c], load_sem.at[1])
    load_a.start()
    near = [c > 0, c + 1 < cols, has_row_below, has_row_above]
    pl.semaphore_wait(barrier, inds - 1 + sum(n.astype(jnp.int32) for n in near))

    def send_x(col, src):
        return remote(src, xs.at[col], xsend.at[col], xrecv.at[col], dev(r, nxt, i))

    def send_w(col, src):
        return remote(src, wl.at[col], wsend.at[col], wrecv.at[col], dev(r, nxt, i))

    def send_n(col, src):
        slot = col - low
        return remote(src, xn.at[slot], nsend.at[slot], nrecv.at[slot], dev(r - 1, c, i))

    def a_up(col, src):
        return remote(src, am.at[0, col], aup.at[col], arecv.at[col], dev(r, c + 1, i))

    def a_down(col, src):
        return remote(src, am.at[0, col], adn.at[col], arecv.at[col], dev(r, c - 1, i))

    def a_cross(col, row):
        return remote(am.at[0, col], am.at[1, col], axs.at[col], crecv.at[col], dev(row, c, i))

    def gives_n(col):
        return has_row_above & is_hub & (col >= low) & (col <= high) & (col < cols - 1)

    when(~is_main, lambda: send_x(c, x_ref).start())
    when(~is_main, lambda: send_w(c, w_ref).start())
    when(gives_n(c), lambda: send_n(c, x_ref).start())
    when(c + 1 < cols, lambda: a_up(c, a_ref).start())
    when(c > 0, lambda: a_down(c, a_ref).start())
    wl[c] = w_ref[...]

    def valid(kind, p, q):
        if kind:
            return has_row_below & (p < q) & ((q >= low) | is_main)
        return jnp.where(last, p >= q, p <= q) & (is_main | ((q >= low) & (q <= high)))

    def away(col):
        return jnp.abs(col - c)

    def ready(kind, p, q):
        return jnp.maximum(away(p) + kind, away(q))

    def reduce_send(kind, l, q, k):
        to = lax.rem(i + k, inds)
        return remote(gp.at[kind, l, q, to], rs.at[k - 1, kind, l, q], ssend.at[kind, l, q, 0, k],
                      rrecv.at[k - 1, kind, l, q], dev(r, c, to))

    def put_tile(kind, l, q):
        value = jnp.dot(xt[kind, l], xs[q], preferred_element_type=jnp.float32)
        gp[kind, l, q] = value.reshape(inds, part, tile)
        loop(1, inds, lambda k: reduce_send(kind, l, q, k).start())

    def use(col, before):
        def turn():
            l = col - low
            xt[0, l] = xs[col].T
            wide = jnp.broadcast_to(wl[col].astype(jnp.float32), (tile, tile))
            wc[l] = wide.T.astype(jnp.int32).reshape(inds, part, tile)

        mine = (col >= low) & (col <= high)
        when(mine, turn)

        def as_q(l):
            p = low + l
            when(((p == col) | before(p)) & (p <= high) & valid(0, p, col),
                 lambda: put_tile(0, l, col))
            when((away(p) + 1 <= away(col)) & (p <= high) & valid(1, p, col),
                 lambda: put_tile(1, l, col))

        loop(0, span, as_q)
        when(mine, lambda: loop(0, cols, lambda q: when(
            before(q) & valid(0, col, q), lambda: put_tile(0, col - low, q))))

    def use_next(col, step):
        l = col - low
        send_n(col, x_ref).wait_recv()
        xt[1, l] = xn[l].T
        loop(0, cols, lambda q: when(
            (away(q) < step) & valid(1, col, q), lambda: put_tile(1, l, q)))

    row_iota = lax.broadcasted_iota(jnp.int32, (part, tile), 0) + i * part
    lane_iota = lax.broadcasted_iota(jnp.int32, (part, tile), 1)

    def s_send(kind, l, q, which, k, row, col, slot):
        to = lax.rem(i + k, inds)
        return remote(sq.at[kind, l, q], sm.at[kind, slot, i], ssend.at[kind, l, q, which, k],
                      srecv.at[kind, slot, i], dev(row, col, to))

    def targets(kind, l, q, act, keep):
        p = low + l
        here = q == c

        def second():
            when(here, keep(q, p))
            first = here.astype(jnp.int32)
            loop(first, inds, lambda k: act(s_send(kind, l, q, 1, k, r, q, p)))

        def same_row():
            when(p == c, keep(p, q))
            first = (p == c).astype(jnp.int32)
            loop(first, inds, lambda k: act(s_send(kind, l, q, 0, k, r, p, q)))

        if kind:
            second()
            loop(0, inds, lambda k: act(s_send(kind, l, q, 0, k, r + 1, p, q)))
        else:
            when(p != q, second)
            same_row()

    def finish(kind, l, q):
        p = low + l
        total = gp[kind, l, q, i]
        for k in range(1, inds):
            reduce_send(kind, l, q, k).wait()
            total = total + rs[k - 1, kind, l, q]
        corr = total / samples
        rsq = corr * corr
        adj = rsq - (1.0 - rsq) / (samples - 2)
        by_lane = jnp.broadcast_to(wl[q], (part, tile))
        if kind:
            pos, lim = ((r + 1) * cols + p) * tile + row_iota, by_lane
        else:
            rows_first = ((p == q) & (lane_iota >= row_iota)) | ((p != q) & ~last)
            pos = jnp.where(rows_first, (r * cols + q) * tile + lane_iota,
                            (r * cols + p) * tile + row_iota)
            lim = jnp.where(rows_first, wc[l, i], by_lane)
        val = jnp.where(pos < lim, adj, 0.0).astype(jnp.bfloat16)
        sq[kind, l, q] = val

        def keep(me, slot):
            def store():
                sm[kind, slot, i] = val
            return store

        targets(kind, l, q, lambda copy: copy.start(), keep)

    def each_tile(fn):
        for kind in range(2):
            def by_l(l, kind=kind):
                def by_q(q):
                    p = low + l
                    when((p <= high) & valid(kind, p, q), lambda: fn(kind, l, q, ready(kind, p, q)))
                loop(0, cols, by_q)
            loop(0, span, by_l)

    def pass_a(s):
        def from_left():
            col = c - s
            a_up(col, am.at[0, col]).wait_recv()
            when(c + 1 < cols, lambda: a_up(col, am.at[0, col]).start())
            when(has_row_above, lambda: a_cross(col, r - 1).start())

        def from_right():
            col = c + s
            a_down(col, am.at[0, col]).wait_recv()
            when(c > 0, lambda: a_down(col, am.at[0, col]).start())
            when(has_row_below, lambda: a_cross(col, r + 1).start())

        when(c - s >= 0, from_left)
        when(c + s < cols, from_right)

    def arrive(col, before):
        send_x(col, xs.at[col]).wait_recv()
        when(~is_main, lambda: send_x(col, xs.at[col]).start())
        when(gives_n(col), lambda: send_n(col, xs.at[col]).start())
        send_w(col, wl.at[col]).wait_recv()
        when(~is_main, lambda: send_w(col, wl.at[col]).start())
        when(is_hub, lambda: use(col, before))

    def needs_n(col):
        return has_row_below & is_hub & (col >= low) & (col <= high) & (col < cols - 1)

    load_x.wait()
    when(is_hub, lambda: use(c, lambda x: x < 0))

    def step(s):
        left, right = c - s + 1, c + s - 1
        when((left >= 0) & needs_n(left), lambda: use_next(left, s))
        when((s > 1) & (right < cols) & needs_n(right), lambda: use_next(right, s))
        left, right = c - s, c + s
        when((left >= 0) & takes_left, lambda: arrive(left, lambda x: away(x) < s))
        when((right < cols) & takes_right, lambda: arrive(
            right, lambda x: (away(x) < s) | (x == c - s)))
        when(is_hub, lambda: each_tile(lambda kind, l, q, t: when(
            t == s - 1, lambda: finish(kind, l, q))))
        when(s < cols, lambda: pass_a(s))

    steps = span + 2
    loop(1, steps, step)
    when(is_hub, lambda: each_tile(lambda kind, l, q, t: when(
        t >= steps - 1, lambda: finish(kind, l, q))))
    loop(steps, cols, pass_a)

    load_a.wait()

    def take(kind, slot, q):
        remote(sq.at[0, 0, 0], sm.at[kind, slot, q], ssend.at[0, 0, 0, 0, 0],
               srecv.at[kind, slot, q], dev(r, c, lax.rem(i + 1, inds))).wait_recv()

    def take_all(kind, slot, p, same_row):
        home = jnp.where(p <= left_hub, left_hub, right_hub)
        first = (same_row & (home == c)).astype(jnp.int32)
        loop(first, inds, lambda k: take(kind, slot, lax.rem(i + k, inds)))

    def add(kind, slot, flip):
        lhs = am[kind, slot]
        rhs = sm[kind, slot].reshape(tile, tile)
        dims = (((1,), (1,)), ((), ())) if flip else (((1,), (0,)), ((), ()))
        o_ref[...] += lax.dot_general(lhs, rhs, dims, preferred_element_type=jnp.float32)

    o_ref[...] = jnp.zeros_like(o_ref)

    def add_row(col):
        p = jnp.where(last, jnp.maximum(c, col), jnp.minimum(c, col))
        take_all(0, col, p, c >= 0)
        when(p == c, lambda: add(0, col, True))
        when(p != c, lambda: add(0, col, False))

    loop(0, cols, add_row)

    def add_cross(col):
        remote(am.at[0, col], am.at[1, col], axs.at[col], crecv.at[col],
               dev(r, nxt, i)).wait_recv()
        take_all(1, col, jnp.minimum(c, col), col < c)
        when(col < c, lambda: add(1, col, False))
        when(col > c, lambda: add(1, col, True))

    when(has_row_below, lambda: loop(0, c, add_cross))
    when(has_row_above, lambda: loop(c + 1, cols, add_cross))

    def sent_x(col):
        send_x(col, xs.at[col]).wait_send()
        send_w(col, wl.at[col]).wait_send()

    when(c < main, lambda: loop(0, c + 1, sent_x))
    when(c > main, lambda: loop(c, cols, sent_x))
    loop(low, high + 1, lambda col: when(
        gives_n(col), lambda: send_n(col, xs.at[col]).wait_send()))
    when(c + 1 < cols, lambda: loop(0, c + 1, lambda q: a_up(q, am.at[0, q]).wait_send()))
    when(c > 0, lambda: loop(c, cols, lambda q: a_down(q, am.at[0, q]).wait_send()))
    when(has_row_above, lambda: loop(0, c, lambda q: a_cross(q, r - 1).wait_send()))
    when(has_row_below, lambda: loop(c + 1, cols, lambda q: a_cross(q, r + 1).wait_send()))

    def drain(kind, l, q, t):
        targets(kind, l, q, lambda copy: copy.wait_send(), lambda me, slot: lambda: None)

    when(is_hub, lambda: each_tile(drain))


def per_device(rows, cols, inds, dosages, annotations, window_end):
    depth, tile = dosages.shape
    ann = annotations.shape[0]
    samples = depth * inds
    part = tile // inds
    span = max(cols // 2, cols - cols // 2)
    dma = pltpu.SemaphoreType.DMA
    sems = (dma((2,)), dma((cols,)), dma((cols,)), dma((span,)), dma((span,)), dma((cols,)),
            dma((cols,)), dma((cols,)), dma((cols,)), dma((cols,)), dma((cols,)), dma((cols,)),
            dma((inds - 1, 2, span, cols)),
            dma((2, span, cols, 2, inds)), dma((2, cols, inds)))
    return pl.pallas_call(
        functools.partial(kernel, rows, cols, inds, samples),
        out_shape=jax.ShapeDtypeStruct((ann, tile), jnp.float32),
        in_specs=[pl.BlockSpec(memory_space=pl.ANY), pl.BlockSpec(memory_space=pl.ANY),
                  pl.BlockSpec(memory_space=pltpu.VMEM)],
        out_specs=pl.BlockSpec(memory_space=pltpu.VMEM),
        scratch_shapes=[
            pltpu.VMEM((cols, depth, tile), jnp.bfloat16),
            pltpu.VMEM((span, depth, tile), jnp.bfloat16),
            pltpu.VMEM((2, span, tile, depth), jnp.bfloat16),
            pltpu.VMEM((cols, 1, tile), jnp.int32),
            pltpu.VMEM((span, inds, part, tile), jnp.int32),
            pltpu.VMEM((2, span, cols, inds, part, tile), jnp.float32),
            pltpu.VMEM((inds - 1, 2, span, cols, part, tile), jnp.float32),
            pltpu.VMEM((2, span, cols, part, tile), jnp.bfloat16),
            pltpu.VMEM((2, cols, inds, part, tile), jnp.bfloat16),
            pltpu.VMEM((2, cols, ann, tile), jnp.bfloat16),
            sems,
        ],
        compiler_params=pltpu.CompilerParams(collective_id=0, has_side_effects=True),
    )(dosages, annotations, window_end.reshape(1, tile))


def solution(mesh):
    in_specs = (P("ind", ("row", "col")), P("ind", ("row", "col")), P(("row", "col")))
    out_specs = P("ind", ("row", "col"))
    body = functools.partial(per_device, mesh.shape["row"], mesh.shape["col"], mesh.shape["ind"])
    return jax.shard_map(body, mesh=mesh, in_specs=in_specs, out_specs=out_specs, check_vma=False)
```

time: 34.3 us -> 33.6 us (0.980)
  the two profiles are of different devices: /device:TPU:0 before, /device:TPU:1 now
where the time goes in v3:
time: 33.6 us; the launch traced here: 33.5 us
  Pallas kernels  31.9 us (95%)
  local copies, waits for them, and re-layouts  1.57 us (5%)
    pallas_call x1, Pallas kernels, per_device(): pl.pallas_call(functools.partial(kernel, rows, cols, inds, samples), out_...  31.9 us
    unnamed x1, local copies, waits for them, and re-layouts  1.57 us

profile of v3, /device:TPU:1, one launch (start us, length us, event | category | flops | bytes accessed | tf_op | source)
XLA Modules:
  0.0 33.5 jit_solution(5592297390802349536)
XLA Ops:
  0.0 31.9 %shard_map.37 = f32[256,128]{1,0:T(8,128)} custom-call(bf16[1024,128]{1,0:T(8,128)(2,1)} %x_ref.1, bf16[256,128]{1,0:T(8,128)(2,1)} %a_ref.1, s32[1,128]{1,0:T(1,128)} %bitcast.1), custom_call_target="tpu_custom_call" | custom-call | tf_op jit(solution)/shard_map/pallas_call | solution.py:329
  31.9 1.6 %copy.5 = f32[256,128]{1,0:T(8,128)} copy(f32[256,128]{1,0:T(8,128)} %shard_map.37) | data formatting | bytes 262144

commit v4 on v3

v4 whole, which is shorter than its diff:
```python
import functools

import jax
import jax.numpy as jnp
from jax import lax
from jax.experimental import pallas as pl
from jax.experimental.pallas import tpu as pltpu
from jax.sharding import PartitionSpec as P

MESH = pl.DeviceIdType.MESH


def kernel(rows, cols, inds, samples, x_ref, a_ref, w_ref, o_ref, xs, xn, xt, wl, wc,
           gp, rs, sq, smq, smp, am, sems):
    (load_sem, xsend, xrecv, nsend, nrecv, wsend, wrecv, aup, adn, axs, arecv, crecv,
     rsend, rrecv, qsend, qrecv, psend, precv) = sems
    r, c, i = lax.axis_index("row"), lax.axis_index("col"), lax.axis_index("ind")
    tile = x_ref.shape[1]
    part = tile // inds
    right_hub = cols // 2
    left_hub = right_hub - 1
    span = max(right_hub, cols - right_hub)
    last = r == rows - 1
    has_row_below = r < rows - 1
    has_row_above = r > 0
    main = jnp.where(last, right_hub, left_hub)
    is_main = c == main
    is_hub = (c == left_hub) | (c == right_hub)
    on_left = c <= left_hub
    low = jnp.where(on_left, 0, right_hub)
    high = jnp.where(on_left, left_hub, cols - 1)
    nxt = jnp.where(c < main, c + 1, c - 1)
    takes_left = c <= main
    takes_right = c >= main

    def dev(row, col, ind):
        return {"row": row, "col": col, "ind": ind}

    def remote(src, dst, send, recv, target):
        return pltpu.make_async_remote_copy(
            src_ref=src, dst_ref=dst, send_sem=send, recv_sem=recv,
            device_id=target, device_id_type=MESH)

    def when(cond, fn):
        pl.when(cond)(fn)

    def loop(lo, hi, fn):
        def body(step, carry):
            fn(step)
            return carry
        lax.fori_loop(lo, hi, body, 0)

    barrier = pltpu.get_barrier_semaphore()

    def greet(row, col, ind):
        pl.semaphore_signal(barrier, inc=1, device_id=dev(row, col, ind), device_id_type=MESH)

    when(c > 0, lambda: greet(r, c - 1, i))
    when(c + 1 < cols, lambda: greet(r, c + 1, i))
    when(has_row_below, lambda: greet(r + 1, c, i))
    when(has_row_above, lambda: greet(r - 1, c, i))
    for k in range(1, inds):
        greet(r, c, lax.rem(i + k, inds))
    load_x = pltpu.make_async_copy(x_ref, xs.at[c], load_sem.at[0])
    load_x.start()
    load_a = pltpu.make_async_copy(a_ref, am.at[0, c], load_sem.at[1])
    load_a.start()
    near = [c > 0, c + 1 < cols, has_row_below, has_row_above]
    pl.semaphore_wait(barrier, inds - 1 + sum(n.astype(jnp.int32) for n in near))

    def send_x(col, src):
        return remote(src, xs.at[col], xsend.at[col], xrecv.at[col], dev(r, nxt, i))

    def send_w(col, src):
        return remote(src, wl.at[col], wsend.at[col], wrecv.at[col], dev(r, nxt, i))

    def send_n(col, src):
        slot = col - low
        return remote(src, xn.at[slot], nsend.at[slot], nrecv.at[slot], dev(r - 1, c, i))

    def a_up(col, src):
        return remote(src, am.at[0, col], aup.at[col], arecv.at[col], dev(r, c + 1, i))

    def a_down(col, src):
        return remote(src, am.at[0, col], adn.at[col], arecv.at[col], dev(r, c - 1, i))

    def a_cross(col, row):
        return remote(am.at[0, col], am.at[1, col], axs.at[col], crecv.at[col], dev(row, c, i))

    def gives_n(col):
        return has_row_above & is_hub & (col >= low) & (col <= high) & (col < cols - 1)

    when(~is_main, lambda: send_x(c, x_ref).start())
    when(~is_main, lambda: send_w(c, w_ref).start())
    when(gives_n(c), lambda: send_n(c, x_ref).start())
    when(c + 1 < cols, lambda: a_up(c, a_ref).start())
    when(c > 0, lambda: a_down(c, a_ref).start())
    wl[c] = w_ref[...]

    def valid(kind, p, q):
        if kind:
            return has_row_below & (p < q)
        return jnp.where(last, p >= q, p <= q)

    def has_q(q):
        return is_main | ((q >= low) & (q <= high))

    def away(col):
        return jnp.abs(col - c)

    def reduce_send(q, k):
        to = lax.rem(i + k, inds)
        return remote(gp.at[q, to], rs.at[k - 1, q], rsend.at[k - 1, q], rrecv.at[k - 1, q],
                      dev(r, c, to))

    def multiply(q):
        depth = xs.shape[1]
        value = jnp.dot(xt[...].reshape(2 * span * tile, depth), xs[q],
                        preferred_element_type=jnp.float32)
        value = value.reshape(2, span, inds, part, tile)
        for to in range(inds):
            gp[q, to] = value[:, :, to]
        for k in range(1, inds):
            reduce_send(q, k).start()

    def turn(col):
        l = col - low
        xt[0, l] = xs[col].T
        wide = jnp.broadcast_to(wl[col].astype(jnp.float32), (tile, tile))
        wc[l] = wide.T.astype(jnp.int32).reshape(inds, part, tile)

    def turn_next(col):
        l = col - low
        send_n(col, x_ref).wait_recv()
        xt[1, l] = xn[l].T

    row_iota = lax.broadcasted_iota(jnp.int32, (part, tile), 0) + i * part
    lane_iota = lax.broadcasted_iota(jnp.int32, (part, tile), 1)
    side = jnp.where(on_left, 0, 1)

    def to_q(q, k):
        return remote(sq.at[q], smq.at[i, :, pl.ds(low, span)], qsend.at[q, k],
                      qrecv.at[i, side], dev(r, q, lax.rem(i + k, inds)))

    def to_p(kind, l, q, k):
        return remote(sq.at[q, kind, l], smp.at[i, kind, q], psend.at[q, kind, l, k],
                      precv.at[i, kind, q], dev(r + kind, low + l, lax.rem(i + k, inds)))

    def sends(q, act):
        loop((q == c).astype(jnp.int32), inds, lambda k: act(to_q(q, k)))
        for kind in range(2):
            for l in range(span):
                p = low + l
                first = 0 if kind else (p == c).astype(jnp.int32)

                def go(kind=kind, l=l, first=first):
                    loop(first, inds, lambda k: act(to_p(kind, l, q, k)))

                when((p != q) & valid(kind, p, q), go)

    def finish(q):
        total = gp[q, i]
        for k in range(1, inds):
            reduce_send(q, k).wait_recv()
            total = total + rs[k - 1, q]
        corr = total / samples
        rsq = corr * corr
        adj = rsq - (1.0 - rsq) / (samples - 2)
        by_lane = jnp.broadcast_to(wl[q], (part, tile))
        for kind in range(2):
            for l in range(span):
                p = low + l
                if kind:
                    pos, lim = ((r + 1) * cols + p) * tile + row_iota, by_lane
                else:
                    rows_first = ((p == q) & (lane_iota >= row_iota)) | ((p != q) & ~last)
                    pos = jnp.where(rows_first, (r * cols + q) * tile + lane_iota,
                                    (r * cols + p) * tile + row_iota)
                    lim = jnp.where(rows_first, wc[l, i], by_lane)
                val = jnp.where(pos < lim, adj[kind, l], 0.0).astype(jnp.bfloat16)
                sq[q, kind, l] = val
        sends(q, lambda copy: copy.start())

        def keep_q():
            smq[i, :, pl.ds(low, span)] = sq[q]

        when(q == c, keep_q)

        def keep_p():
            smp[i, 0, q] = sq[q, 0, c - low]

        when(q != c, keep_p)

    def pass_a(s):
        def from_left():
            col = c - s
            a_up(col, am.at[0, col]).wait_recv()
            when(c + 1 < cols, lambda: a_up(col, am.at[0, col]).start())
            when(has_row_above, lambda: a_cross(col, r - 1).start())

        def from_right():
            col = c + s
            a_down(col, am.at[0, col]).wait_recv()
            when(c > 0, lambda: a_down(col, am.at[0, col]).start())
            when(has_row_below, lambda: a_cross(col, r + 1).start())

        when(c - s >= 0, from_left)
        when(c + s < cols, from_right)

    def in_l(col):
        return is_hub & (col >= low) & (col <= high)

    def arrive(col):
        send_x(col, xs.at[col]).wait_recv()
        when(~is_main, lambda: send_x(col, xs.at[col]).start())
        when(gives_n(col), lambda: send_n(col, xs.at[col]).start())
        send_w(col, wl.at[col]).wait_recv()
        when(~is_main, lambda: send_w(col, wl.at[col]).start())
        when(in_l(col), lambda: turn(col))

    def arrivals(s):
        left, right = c - s, c + s
        when((left >= 0) & takes_left, lambda: arrive(left))
        when((right < cols) & takes_right, lambda: arrive(right))

    def each_q(cond, fn):
        when(is_hub, lambda: loop(0, cols, lambda q: when(
            has_q(q) & cond(away(q)), lambda: fn(q))))

    load_x.wait()
    when(is_hub, lambda: turn(c))

    def step(s):
        arrivals(s)
        pass_a(s)

    loop(1, span, step)
    loop(low, high + 1, lambda col: when(
        in_l(col) & has_row_below & (col < cols - 1), lambda: turn_next(col)))
    each_q(lambda d: d < span, multiply)
    arrivals(span)
    each_q(lambda d: d >= span, multiply)
    loop(span, cols, pass_a)
    each_q(lambda d: d < span, finish)
    each_q(lambda d: d >= span, finish)

    load_a.wait()

    def take_q(which):
        home = jnp.where(which == 0, left_hub, right_hub)
        first = (home == c).astype(jnp.int32)
        loop(first, inds, lambda k: remote(
            sq.at[0], smq.at[lax.rem(i + k, inds), :, pl.ds(which * right_hub, span)],
            qsend.at[0, 0], qrecv.at[lax.rem(i + k, inds), which], dev(r, c, i)).wait_recv())

    def take_p(kind, q, first):
        loop(first, inds, lambda k: remote(
            sq.at[0, 0, 0], smp.at[lax.rem(i + k, inds), kind, q], psend.at[0, 0, 0, 0],
            precv.at[lax.rem(i + k, inds), kind, q], dev(r, c, i)).wait_recv())

    def add(lhs, rhs, axis):
        o_ref[...] += lax.dot_general(lhs, rhs.reshape(tile, tile), (((1,), (axis,)), ((), ())),
                                      preferred_element_type=jnp.float32)

    o_ref[...] = jnp.zeros_like(o_ref)
    hub_first = is_hub.astype(jnp.int32)

    def as_p(q):
        take_p(0, q, hub_first)
        add(am[0, q], smp[:, 0, q], 1)

    loop(jnp.where(last, 0, c + 1), jnp.where(last, c, cols), as_p)

    def wait_cross(col):
        remote(am.at[0, col], am.at[1, col], axs.at[col], crecv.at[col],
               dev(r, nxt, i)).wait_recv()

    def as_next_p(q):
        wait_cross(q)
        take_p(1, q, 0)
        add(am[1, q], smp[:, 1, q], 1)

    when(has_row_above, lambda: loop(c + 1, cols, as_next_p))
    when(~last, lambda: take_q(0))
    when(~last & ~on_left, lambda: take_q(1))
    when(last, lambda: take_q(1))
    when(last & on_left, lambda: take_q(0))
    loop(jnp.where(last, c, 0), jnp.where(last, cols, c + 1),
         lambda p: add(am[0, p], smq[:, 0, p], 0))

    def as_q_cross(p):
        wait_cross(p)
        add(am[1, p], smq[:, 1, p], 0)

    when(has_row_below, lambda: loop(0, c, as_q_cross))

    def sent_x(col):
        send_x(col, xs.at[col]).wait_send()
        send_w(col, wl.at[col]).wait_send()

    when(c < main, lambda: loop(0, c + 1, sent_x))
    when(c > main, lambda: loop(c, cols, sent_x))
    loop(low, high + 1, lambda col: when(
        gives_n(col), lambda: send_n(col, xs.at[col]).wait_send()))
    when(c + 1 < cols, lambda: loop(0, c + 1, lambda q: a_up(q, am.at[0, q]).wait_send()))
    when(c > 0, lambda: loop(c, cols, lambda q: a_down(q, am.at[0, q]).wait_send()))
    when(has_row_above, lambda: loop(0, c, lambda q: a_cross(q, r - 1).wait_send()))
    when(has_row_below, lambda: loop(c + 1, cols, lambda q: a_cross(q, r + 1).wait_send()))

    def drain(q):
        for k in range(1, inds):
            reduce_send(q, k).wait_send()
        sends(q, lambda copy: copy.wait_send())

    each_q(lambda d: d >= 0, drain)


def per_device(rows, cols, inds, dosages, annotations, window_end):
    depth, tile = dosages.shape
    ann = annotations.shape[0]
    samples = depth * inds
    part = tile // inds
    span = max(cols // 2, cols - cols // 2)
    dma = pltpu.SemaphoreType.DMA
    sems = (dma((2,)), dma((cols,)), dma((cols,)), dma((span,)), dma((span,)), dma((cols,)),
            dma((cols,)), dma((cols,)), dma((cols,)), dma((cols,)), dma((cols,)), dma((cols,)),
            dma((inds - 1, cols)), dma((inds - 1, cols)), dma((cols, inds)), dma((inds, 2)),
            dma((cols, 2, span, inds)), dma((inds, 2, cols)))
    return pl.pallas_call(
        functools.partial(kernel, rows, cols, inds, samples),
        out_shape=jax.ShapeDtypeStruct((ann, tile), jnp.float32),
        in_specs=[pl.BlockSpec(memory_space=pl.ANY), pl.BlockSpec(memory_space=pl.ANY),
                  pl.BlockSpec(memory_space=pltpu.VMEM)],
        out_specs=pl.BlockSpec(memory_space=pltpu.VMEM),
        scratch_shapes=[
            pltpu.VMEM((cols, depth, tile), jnp.bfloat16),
            pltpu.VMEM((span, depth, tile), jnp.bfloat16),
            pltpu.VMEM((2, span, tile, depth), jnp.bfloat16),
            pltpu.VMEM((cols, 1, tile), jnp.int32),
            pltpu.VMEM((span, inds, part, tile), jnp.int32),
            pltpu.VMEM((cols, inds, 2, span, part, tile), jnp.float32),
            pltpu.VMEM((inds - 1, cols, 2, span, part, tile), jnp.float32),
            pltpu.VMEM((cols, 2, span, part, tile), jnp.bfloat16),
            pltpu.VMEM((inds, 2, cols, part, tile), jnp.bfloat16),
            pltpu.VMEM((inds, 2, cols, part, tile), jnp.bfloat16),
            pltpu.VMEM((2, cols, ann, tile), jnp.bfloat16),
            sems,
        ],
        compiler_params=pltpu.CompilerParams(collective_id=0, has_side_effects=True),
    )(dosages, annotations, window_end.reshape(1, tile))


def solution(mesh):
    in_specs = (P("ind", ("row", "col")), P("ind", ("row", "col")), P(("row", "col")))
    out_specs = P("ind", ("row", "col"))
    body = functools.partial(per_device, mesh.shape["row"], mesh.shape["col"], mesh.shape["ind"])
    return jax.shard_map(body, mesh=mesh, in_specs=in_specs, out_specs=out_specs, check_vma=False)
```

time: 33.6 us -> 34.9 us (1.039)
  Pallas kernels: 31.9 us -> 33.1 us
    pallas_call x1, Pallas kernels: 31.9 us -> 33.1 us  [per_device(): pl.pallas_call(functools.partial(kernel, rows, cols, inds, samples), out_...]
where the time goes in v4:
time: 34.9 us; the launch traced here: 34.7 us
  Pallas kernels  33.1 us (95%)
  local copies, waits for them, and re-layouts  1.57 us (4%)
    pallas_call x1, Pallas kernels, per_device(): pl.pallas_call(functools.partial(kernel, rows, cols, inds, samples), out_...  33.1 us
    unnamed x1, local copies, waits for them, and re-layouts  1.57 us

profile of v4, /device:TPU:1, one launch (start us, length us, event | category | flops | bytes accessed | tf_op | source)
XLA Modules:
  0.0 34.7 jit_solution(5023529525361770033)
XLA Ops:
  0.0 33.1 %shard_map.37 = f32[256,128]{1,0:T(8,128)} custom-call(bf16[1024,128]{1,0:T(8,128)(2,1)} %x_ref.1, bf16[256,128]{1,0:T(8,128)(2,1)} %a_ref.1, s32[1,128]{1,0:T(1,128)} %bitcast.1), custom_call_target="tpu_custom_call" | custom-call | tf_op jit(solution)/shard_map/pallas_call | solution.py:329
  33.2 1.6 %copy.5 = f32[256,128]{1,0:T(8,128)} copy(f32[256,128]{1,0:T(8,128)} %shard_map.37) | data formatting | bytes 262144

commit v5 on v3

--- a/solution.py
+++ b/solution.py
@@ -68,8 +68,13 @@
     near = [c > 0, c + 1 < cols, has_row_below, has_row_above]
     pl.semaphore_wait(barrier, inds - 1 + sum(n.astype(jnp.int32) for n in near))
 
-    def send_x(col, src):
-        return remote(src, xs.at[col], xsend.at[col], xrecv.at[col], dev(r, nxt, i))
+    pieces = 4
+    piece = x_ref.shape[0] // pieces
+
+    def send_x(col, src, h):
+        at = pl.ds(h * piece, piece)
+        return remote(src.at[at], xs.at[col, at], xsend.at[col, h], xrecv.at[col, h],
+                      dev(r, nxt, i))
 
     def send_w(col, src):
         return remote(src, wl.at[col], wsend.at[col], wrecv.at[col], dev(r, nxt, i))
@@ -90,11 +95,12 @@
     def gives_n(col):
         return has_row_above & is_hub & (col >= low) & (col <= high) & (col < cols - 1)
 
-    when(~is_main, lambda: send_x(c, x_ref).start())
+    when(c + 1 < cols, lambda: a_up(c, a_ref).start())
+    when(c > 0, lambda: a_down(c, a_ref).start())
+    for h in range(pieces):
+        when(~is_main, lambda h=h: send_x(c, x_ref, h).start())
     when(~is_main, lambda: send_w(c, w_ref).start())
     when(gives_n(c), lambda: send_n(c, x_ref).start())
-    when(c + 1 < cols, lambda: a_up(c, a_ref).start())
-    when(c > 0, lambda: a_down(c, a_ref).start())
     wl[c] = w_ref[...]
 
     def valid(kind, p, q):
@@ -228,8 +234,9 @@
         when(c + s < cols, from_right)
 
     def arrive(col, before):
-        send_x(col, xs.at[col]).wait_recv()
-        when(~is_main, lambda: send_x(col, xs.at[col]).start())
+        for h in range(pieces):
+            send_x(col, xs.at[col], h).wait_recv()
+            when(~is_main, lambda h=h: send_x(col, xs.at[col], h).start())
         when(gives_n(col), lambda: send_n(col, xs.at[col]).start())
         send_w(col, wl.at[col]).wait_recv()
         when(~is_main, lambda: send_w(col, wl.at[col]).start())
@@ -245,13 +252,13 @@
         left, right = c - s + 1, c + s - 1
         when((left >= 0) & needs_n(left), lambda: use_next(left, s))
         when((s > 1) & (right < cols) & needs_n(right), lambda: use_next(right, s))
+        when(s < cols, lambda: pass_a(s))
         left, right = c - s, c + s
         when((left >= 0) & takes_left, lambda: arrive(left, lambda x: away(x) < s))
         when((right < cols) & takes_right, lambda: arrive(
             right, lambda x: (away(x) < s) | (x == c - s)))
         when(is_hub, lambda: each_tile(lambda kind, l, q, t: when(
             t == s - 1, lambda: finish(kind, l, q))))
-        when(s < cols, lambda: pass_a(s))
 
     steps = span + 2
     loop(1, steps, step)
@@ -297,7 +304,8 @@
     when(has_row_above, lambda: loop(c + 1, cols, add_cross))
 
     def sent_x(col):
-        send_x(col, xs.at[col]).wait_send()
+        for h in range(pieces):
+            send_x(col, xs.at[col], h).wait_send()
         send_w(col, wl.at[col]).wait_send()
 
     when(c < main, lambda: loop(0, c + 1, sent_x))
@@ -322,7 +330,7 @@
     part = tile // inds
     span = max(cols // 2, cols - cols // 2)
     dma = pltpu.SemaphoreType.DMA
-    sems = (dma((2,)), dma((cols,)), dma((cols,)), dma((span,)), dma((span,)), dma((cols,)),
+    sems = (dma((2,)), dma((cols, 4)), dma((cols, 4)), dma((span,)), dma((span,)), dma((cols,)),
             dma((cols,)), dma((cols,)), dma((cols,)), dma((cols,)), dma((cols,)), dma((cols,)),
             dma((inds - 1, 2, span, cols)),
             dma((2, span, cols, 2, inds)), dma((2, cols, inds)))

time: 33.6 us -> 31.6 us (0.940)
  Pallas kernels: 31.9 us -> 29.8 us
    pallas_call x1, Pallas kernels: 31.9 us -> 29.8 us  [per_device(): pl.pallas_call(functools.partial(kernel, rows, cols, inds, samples), out_...]
where the time goes in v5:
time: 31.6 us; the launch traced here: 31.4 us
  Pallas kernels  29.8 us (94%)
  local copies, waits for them, and re-layouts  1.57 us (5%)
    pallas_call x1, Pallas kernels, per_device(): pl.pallas_call(functools.partial(kernel, rows, cols, inds, samples), out_...  29.8 us
    unnamed x1, local copies, waits for them, and re-layouts  1.57 us

profile of v5, /device:TPU:1, one launch (start us, length us, event | category | flops | bytes accessed | tf_op | source)
XLA Modules:
  0.0 31.4 jit_solution(473028223361136746)
XLA Ops:
  0.0 29.8 %shard_map.37 = f32[256,128]{1,0:T(8,128)} custom-call(bf16[1024,128]{1,0:T(8,128)(2,1)} %x_ref.1, bf16[256,128]{1,0:T(8,128)(2,1)} %a_ref.1, s32[1,128]{1,0:T(1,128)} %bitcast.1), custom_call_target="tpu_custom_call" | custom-call | tf_op jit(solution)/shard_map/pallas_call | solution.py:337
  29.8 1.6 %copy.5 = f32[256,128]{1,0:T(8,128)} copy(f32[256,128]{1,0:T(8,128)} %shard_map.37) | data formatting | bytes 262144
